TPU v7x, 256 devices: a whole 4x4x8 slice. The times are simulated.
256 devices in a mesh: span: 4 (over x), seq: 64 (over y, z, core).
Axes of the slice: x: 4, y: 4, z: 8, core: 2. Of those that a mesh axis runs over, the one named last changes fastest.
Arguments:
- query_rows: bfloat16 [4, 14336, 3072], P('span', 'seq'), may hold values from -10 to 10
- key_rows: bfloat16 [4, 14336, 512], P('span', 'seq'), may hold values from -10 to 10
- value_rows: bfloat16 [4, 14336, 512], P('span', 'seq'), may hold values from -6 to 6
- owner_ids: int32 [4, 14336], P('span', 'seq'), may hold values from 0 to 63, as said below
Outputs:
- attended: bfloat16 [4, 14336, 3072], P('span', 'seq')
Inputs may be any that keep to these rules, and one draw needn't show every extreme that they name: `owner_ids`: from the rows of one device at most 7 go to any one owner; in every time span one owner receives exactly 7 rows from every device of its span, and no owner more than 448 rows in all.
All inputs are finite; a program needn't handle non-finite values.
Results may differ from a plain program's by a relative error of at most 0.0055.
Values may be sent and summed in bfloat16 or wider, within the bound.
No kernel may reach another device: no remote copies, remote signals or barrier semaphores. Data moves between devices by JAX's collectives and lax.ppermute only.
A program may use at most 128 MiB of HBM per device.

v0:
```python
import functools
import math

import jax
import jax.numpy as jnp
from jax import lax
from jax.experimental import pallas as pl
from jax.experimental.pallas import tpu as pltpu
from jax.sharding import PartitionSpec as P

HQ = 24
KVH = 4
HD = 128
GROUP = HQ // KVH
TILE = 8
SLOTS = 7
WIDE = SLOTS * HD
BACK = GROUP * HD
KEY_BLOCK = 256
QUERY_BLOCK = 128
ALIGN = 16
EMPTY = 2.0**100
F32 = jnp.float32
BF16 = jnp.bfloat16
VMEM_LIMIT = 48 << 20
PACK_LIMIT = 58 << 20


def iota(shape, dim):
    return lax.broadcasted_iota(jnp.int32, shape, dim)


def row_ranks(owner_ref, axis):
    count = owner_ref.shape[1]
    along = jnp.broadcast_to(owner_ref[...].astype(F32), (count, count))
    down = along.T
    earlier = (along == down) & (iota((count, count), axis) < iota((count, count), 1 - axis))
    rank = jnp.sum(jnp.where(earlier, 1.0, 0.0), axis=axis, keepdims=True)
    owner = owner_ref[...] if axis == 0 else down[:, :1].astype(jnp.int32)
    return owner, rank.astype(jnp.int32)


def one_hot(condition):
    return jnp.where(condition, 1.0, 0.0).astype(BF16)


def pack_kernel(
    owner_ref, query_hbm, key_hbm, value_hbm, out_hbm, query_ref, key_ref, value_ref, out_ref, sem, out_sem
):
    pairs = ((value_hbm, value_ref), (key_hbm, key_ref), (query_hbm, query_ref))
    copies = [pltpu.make_async_copy(source, target, sem.at[i]) for i, (source, target) in enumerate(pairs)]
    for copy in copies:
        copy.start()
    owner, rank = row_ranks(owner_ref, 0)
    count = owner.shape[1]
    rows = out_ref.shape[1]
    place = iota((rows, count), 0)
    chosen = jnp.where(place == owner * TILE + rank, 1.0, 0.0)
    filled = jnp.sum(chosen, axis=1, keepdims=True)
    slot = (iota((rows, 1), 0) & (TILE - 1)) < SLOTS
    mark = jnp.where(slot & (filled == 0.0), F32(EMPTY), F32(0.0))
    select = chosen.astype(BF16)
    spare = place == owner * TILE + SLOTS
    copies[0].wait()
    tails = [
        jnp.dot(one_hot(spare & (rank == k)), value_ref[...], preferred_element_type=F32) for k in range(SLOTS)
    ]
    copies[1].wait()
    copies[2].wait()
    leaving = []
    for c in range(KVH):
        own = slice(c * HD, (c + 1) * HD)
        keys = jnp.dot(select, key_ref[:, own], preferred_element_type=F32)
        out_ref[c, :, :HD] = (keys + mark + tails[0][:, own]).astype(BF16)
        queries = jnp.dot(select, query_ref[:, c * BACK : (c + 1) * BACK], preferred_element_type=F32)
        rest = jnp.concatenate([tails[k][:, own] for k in range(1, SLOTS)], axis=1)
        out_ref[c, :, HD:] = (queries + rest).astype(BF16)
        leave = pltpu.make_async_copy(out_ref.at[c], out_hbm.at[pl.ds(c * rows, rows), :], out_sem.at[c])
        leave.start()
        leaving.append(leave)
    for leave in leaving:
        leave.wait()


def spread_tail(spare_rows):
    tiles = spare_rows.shape[0]
    sub = iota((tiles, TILE, HD), 1)
    tail = jnp.zeros((tiles, TILE, HD), F32)
    for k in range(SLOTS):
        piece = jnp.broadcast_to(spare_rows[:, :, k * HD : (k + 1) * HD], (tiles, TILE, HD))
        tail = jnp.where(sub == k, piece, tail)
    return tail.reshape(tiles * TILE, HD)


def attend_kernel(
    got_ref, out_ref, x_ref, before_ref, k_ref, v_ref, turned_ref, bias_ref, query_ref, held_ref, score_ref, sem
):
    spans = x_ref.shape[0]
    rows = x_ref.shape[1]
    blocks = query_ref.shape[0]
    lanes = GROUP * QUERY_BLOCK
    factor = F32(math.log2(math.e) / math.sqrt(HD))

    def arrival(t):
        source = got_ref.at[pl.ds(pl.multiple_of(t * rows, rows), rows), :]
        return pltpu.make_async_copy(source, x_ref.at[t, :, pl.ds(0, WIDE)], sem.at[t])

    for t in range(spans):
        arrival(t).start()
    before_ref[...] = one_hot(iota((rows, rows), 1) < iota((rows, rows), 0))
    k_ref[...] = jnp.zeros_like(k_ref)
    v_ref[...] = jnp.zeros_like(v_ref)
    bias_ref[...] = jnp.full(bias_ref.shape, -1e30, F32)

    def span_step(t, offset):
        arrival(t).wait()
        spare_rows = x_ref[t, :, :WIDE].astype(F32).reshape(rows // TILE, TILE, WIDE)[:, SLOTS:, :]
        x_ref[t, :, WIDE:] = spread_tail(spare_rows).astype(BF16)
        marks = x_ref[t, :, :HD].astype(F32)
        valid = (marks < F32(EMPTY / 2)) & ((iota((rows, HD), 0) & (TILE - 1)) < SLOTS)
        ahead = jnp.dot(before_ref[...], one_hot(valid), preferred_element_type=F32)
        down = jnp.where(valid, ahead, -1.0)
        along = down.T[:1].astype(jnp.int32)
        total = (jnp.max(down) + 1.0).astype(jnp.int32)
        count = (total + QUERY_BLOCK - 1) // QUERY_BLOCK

        def gather_block(i, _):
            fold = one_hot(iota((QUERY_BLOCK, rows), 0) + i * QUERY_BLOCK == along)
            dense = jnp.dot(fold, x_ref[t], preferred_element_type=F32)
            at = pl.ds(pl.multiple_of(offset + i * QUERY_BLOCK, ALIGN), QUERY_BLOCK)
            k_ref[at, :] = dense[:, :HD].astype(BF16)
            v_ref[at, :] = dense[:, WIDE:]
            inside = iota((QUERY_BLOCK, HD), 0) + i * QUERY_BLOCK < total
            bias_ref[at, :] = jnp.where(inside, F32(0.0), F32(-1e30))
            stack = jnp.concatenate([dense[:, (1 + h) * HD : (2 + h) * HD] for h in range(GROUP)], axis=0)
            query_ref[i] = stack.T.astype(BF16)
            return 0

        lax.fori_loop(0, count, gather_block, 0)
        end = offset + total

        def turn_block(b, _):
            at = pl.ds(pl.multiple_of(b * KEY_BLOCK, KEY_BLOCK), KEY_BLOCK)
            turned_ref[:, at] = v_ref[at, :].T.astype(BF16)
            return 0

        key_blocks = (end + KEY_BLOCK - 1) // KEY_BLOCK
        lax.fori_loop(offset // KEY_BLOCK, key_blocks, turn_block, 0)

        def attend_block(i, used):
            at = pl.ds(pl.multiple_of(i * QUERY_BLOCK, QUERY_BLOCK), QUERY_BLOCK)
            top = jnp.full((1, lanes), -1e30, F32)
            for b in range(used):
                part = slice(b * KEY_BLOCK, (b + 1) * KEY_BLOCK)
                bias = jnp.concatenate([bias_ref[part, :]] * (lanes // HD), axis=1)
                scores = jnp.dot(k_ref[part, :], query_ref[i], preferred_element_type=F32) * factor + bias
                score_ref[part, :] = scores
                top = jnp.maximum(top, jnp.max(scores, axis=0, keepdims=True))
            total = jnp.zeros((1, lanes), F32)
            accum = jnp.zeros((HD, lanes), F32)
            for b in range(used):
                part = slice(b * KEY_BLOCK, (b + 1) * KEY_BLOCK)
                weights = jnp.exp2(score_ref[part, :] - top)
                total = total + jnp.sum(weights, axis=0, keepdims=True)
                accum = accum + jnp.dot(turned_ref[:, part], weights.astype(BF16), preferred_element_type=F32)
            result = (accum / total).T.astype(BF16)
            for h in range(GROUP):
                held_ref[at, h * HD : (h + 1) * HD] = result[h * QUERY_BLOCK : (h + 1) * QUERY_BLOCK]

        def query_step(i, _):
            for used in range(1, turned_ref.shape[1] // KEY_BLOCK + 1):
                pl.when(key_blocks == used)(functools.partial(attend_block, i, used))
            return 0

        lax.fori_loop(0, count, query_step, 0)

        def clear_block(i, _):
            at = pl.ds(pl.multiple_of(i * QUERY_BLOCK, QUERY_BLOCK), QUERY_BLOCK)
            held_ref[at, :] = jnp.zeros((QUERY_BLOCK, BACK), BF16)
            return 0

        lax.fori_loop(count, blocks, clear_block, 0)
        slots = blocks * QUERY_BLOCK
        wide = jnp.concatenate([down] * (-(-slots // HD)), axis=1)[:, :slots]
        unfold = one_hot(wide == iota((rows, slots), 1).astype(F32))
        moved = jnp.dot(unfold, held_ref[...], preferred_element_type=F32)
        out_ref[pl.ds(pl.multiple_of(t * rows, rows), rows), :] = moved.astype(BF16)
        return offset + (total + ALIGN - 1) // ALIGN * ALIGN

    lax.fori_loop(0, spans, span_step, jnp.int32(0))


def unpack_kernel(owner_ref, got_ref, out_ref):
    owner, rank = row_ranks(owner_ref, 1)
    count = owner.shape[0]
    rows = got_ref.shape[0] // KVH
    pick = one_hot(iota((count, rows), 1) == owner * TILE + rank)
    for c in range(KVH):
        moved = jnp.dot(pick, got_ref[c * rows : (c + 1) * rows, :], preferred_element_type=F32)
        out_ref[:, c * BACK : (c + 1) * BACK] = moved.astype(BF16)


def call(kernel, name, out_shape, flops, moved, scratch=(), limit=VMEM_LIMIT, **specs):
    return pl.pallas_call(
        kernel,
        out_shape=out_shape,
        scratch_shapes=list(scratch),
        compiler_params=pltpu.CompilerParams(vmem_limit_bytes=limit),
        cost_estimate=pl.CostEstimate(flops=flops, bytes_accessed=moved, transcendentals=0),
        name=name,
        **specs,
    )


def exchange(rows):
    shaped = rows.reshape(rows.shape[0] // TILE, TILE, rows.shape[1])
    return lax.all_to_all(shaped, ("span", "seq"), split_axis=0, concat_axis=0, tiled=True).reshape(rows.shape)


def attend(got, owners, spans):
    rows = owners * TILE
    own_rows = owners * SLOTS
    key_blocks = -(-(spans * own_rows + QUERY_BLOCK) // KEY_BLOCK)
    key_rows = key_blocks * KEY_BLOCK
    return call(
        attend_kernel,
        "attend",
        jax.ShapeDtypeStruct((spans * rows, BACK), BF16),
        4 * own_rows * own_rows * spans * spans * HD * GROUP,
        4 * spans * rows * WIDE,
        [
            pltpu.VMEM((spans, rows, WIDE + HD), BF16),
            pltpu.VMEM((rows, rows), BF16),
            pltpu.VMEM((key_rows, HD), BF16),
            pltpu.VMEM((key_rows, HD), F32),
            pltpu.VMEM((HD, key_rows), BF16),
            pltpu.VMEM((key_rows, HD), F32),
            pltpu.VMEM((-(-own_rows // QUERY_BLOCK), HD, GROUP * QUERY_BLOCK), BF16),
            pltpu.VMEM((-(-own_rows // QUERY_BLOCK) * QUERY_BLOCK, BACK), BF16),
            pltpu.VMEM((key_rows, GROUP * QUERY_BLOCK), F32),
            pltpu.SemaphoreType.DMA((spans,)),
        ],
        in_specs=[pl.BlockSpec(memory_space=pl.ANY)],
    )(got)


def local(query_rows, key_rows, value_rows, owner_ids):
    owners = lax.axis_size("seq")
    spans = lax.axis_size("span")
    row_count = query_rows.shape[1]
    rows = owners * TILE
    shape = jax.ShapeDtypeStruct
    send = call(
        pack_kernel,
        "pack",
        shape((KVH * rows, WIDE), BF16),
        4 * rows * row_count * HQ * HD,
        8 * rows * WIDE,
        [
            pltpu.VMEM((row_count, HQ * HD), BF16),
            pltpu.VMEM((row_count, KVH * HD), BF16),
            pltpu.VMEM((row_count, KVH * HD), BF16),
            pltpu.VMEM((KVH, rows, WIDE), BF16),
            pltpu.SemaphoreType.DMA((3,)),
            pltpu.SemaphoreType.DMA((KVH,)),
        ],
        limit=PACK_LIMIT,
        in_specs=[pl.BlockSpec(memory_space=pltpu.VMEM)] + [pl.BlockSpec(memory_space=pl.ANY)] * 3,
        out_specs=pl.BlockSpec(memory_space=pl.ANY),
    )(owner_ids, query_rows[0], key_rows[0], value_rows[0])
    done = attend(exchange(send), owners, spans)
    result = call(
        unpack_kernel,
        "unpack",
        shape((row_count, HQ * HD), BF16),
        2 * rows * row_count * HQ * HD,
        4 * rows * HQ * HD,
    )(owner_ids, exchange(done))
    return result[None]


def solution(mesh):
    return jax.shard_map(
        local,
        mesh=mesh,
        in_specs=(
            P("span", "seq", None),
            P("span", "seq", None),
            P("span", "seq", None),
            P("span", "seq"),
        ),
        out_specs=P("span", "seq", None),
        check_vma=False,
    )
```

profile of v0, /device:TPU:7, one launch (start us, length us, event | category | flops | bytes accessed | tf_op | source)
XLA Modules:
  0.0 216.4 jit_solution(5856337575695202373)
XLA Ops:
  0.0 5.0 %pack.1 = bf16[2048,896]{1,0:T(8,128)(2,1)} custom-call(s32[1,224]{1,0:T(1,128)} %owner_ref.3, bf16[224,3072]{1,0:T(8,128)(2,1)} %bitcast.12, bf16[224,512]{1,0:T(8,128)(2,1)} %bitcast.13, bf16[224,512]{1,0:T(8,128)(2,1)} %bitcast.14), custom_call_target="tpu_custom_call" | custom-call | flops 1409286144 | bytes 3670016 | tf_op jit(solution)/shard_map/pack/pallas_call | solution.py:253
  5.0 101.8 %all_to_all.10 = bf16[256,8,896]{2,1,0:T(8,128)(2,1)} all-to-all(bf16[256,8,896]{2,1,0:T(8,128)(2,1)} %bitcast.10), channel_id=1, replica_groups=mesh['span'=4,'seq'=64] {'span','seq'}, dimensions={0} | all-to-all | bytes 7340032 | tf_op jit(solution)/shard_map/all_to_all | solution.py:217
  106.9 21.2 %attend.1 = bf16[2048,768]{1,0:T(8,128)(2,1)S(1)} custom-call(bf16[2048,896]{1,0:T(8,128)(2,1)} %bitcast.11), custom_call_target="tpu_custom_call" | custom-call | flops 9865003008 | bytes 7340032 | tf_op jit(solution)/shard_map/attend/pallas_call | solution.py:225
  128.1 0.0 copy-start
  128.1 86.1 %all_to_all.11 = bf16[256,8,768]{2,1,0:T(8,128)(2,1)S(1)} all-to-all(bf16[256,8,768]{2,1,0:T(8,128)(2,1)S(1)} %bitcast.9), channel_id=1, replica_groups=mesh['span'=4,'seq'=64] {'span','seq'}, dimensions={0} | all-to-all | bytes 6291456 | tf_op jit(solution)/shard_map/all_to_all | solution.py:217
  214.2 0.0 copy-done
  214.2 2.2 %unpack.1 = bf16[224,3072]{1,0:T(8,128)(2,1)} custom-call(s32[1,224]{1,0:T(1,128)S(1)} %copy-done, bf16[2048,768]{1,0:T(8,128)(2,1)S(1)} %bitcast.8), custom_call_target="tpu_custom_call" | custom-call | flops 704643072 | bytes 6291456 | tf_op jit(solution)/shard_map/unpack/pallas_call | solution.py:272
Async XLA Ops:
  128.1 86.1 %copy-start = (s32[1,224]{1,0:T(1,128)S(1)}, s32[1,224]{1,0:T(1,128)}, u32[]{:S(2)}) copy-start(s32[1,224]{1,0:T(1,128)} %owner_ref.3) | copy-start | bytes 2692
where the time goes:
time: 218 us; the launch traced here: 216 us
  blocking collectives  188 us (86%)
  Pallas kernels  28.5 us (13%)
    all_to_all x2, blocking collectives, exchange(): lax.all_to_all(shaped, ('span', 'seq'), split_axis=0, concat_axis=0, tile...  188 us
    pallas_call x1, Pallas kernels, attend(): call(attend_kernel, 'attend', jax.ShapeDtypeStruct((spans * rows, BACK),...  21.2 us
    pallas_call x1, Pallas kernels, local(): call(pack_kernel, 'pack', shape((KVH * rows, WIDE), BF16), 4 * rows * row...  5.03 us

commit v1 on v0

--- a/solution.py
+++ b/solution.py
@@ -18,6 +18,7 @@
 BACK = GROUP * HD
 KEY_BLOCK = 256
 QUERY_BLOCK = 128
+HALF_BLOCK = QUERY_BLOCK // 2
 ALIGN = 16
 EMPTY = 2.0**100
 F32 = jnp.float32
@@ -98,7 +99,6 @@
     spans = x_ref.shape[0]
     rows = x_ref.shape[1]
     blocks = query_ref.shape[0]
-    lanes = GROUP * QUERY_BLOCK
     factor = F32(math.log2(math.e) / math.sqrt(HD))
 
     def arrival(t):
@@ -122,21 +122,27 @@
         down = jnp.where(valid, ahead, -1.0)
         along = down.T[:1].astype(jnp.int32)
         total = (jnp.max(down) + 1.0).astype(jnp.int32)
-        count = (total + QUERY_BLOCK - 1) // QUERY_BLOCK
-
-        def gather_block(i, _):
-            fold = one_hot(iota((QUERY_BLOCK, rows), 0) + i * QUERY_BLOCK == along)
+        halves = (total + HALF_BLOCK - 1) // HALF_BLOCK
+        count = halves // 2
+        odd = halves % 2 == 1
+
+        def gather_block(size, i):
+            fold = one_hot(iota((size, rows), 0) + i * QUERY_BLOCK == along)
             dense = jnp.dot(fold, x_ref[t], preferred_element_type=F32)
-            at = pl.ds(pl.multiple_of(offset + i * QUERY_BLOCK, ALIGN), QUERY_BLOCK)
+            at = pl.ds(pl.multiple_of(offset + i * QUERY_BLOCK, ALIGN), size)
             k_ref[at, :] = dense[:, :HD].astype(BF16)
             v_ref[at, :] = dense[:, WIDE:]
-            inside = iota((QUERY_BLOCK, HD), 0) + i * QUERY_BLOCK < total
+            inside = iota((size, HD), 0) + i * QUERY_BLOCK < total
             bias_ref[at, :] = jnp.where(inside, F32(0.0), F32(-1e30))
             stack = jnp.concatenate([dense[:, (1 + h) * HD : (2 + h) * HD] for h in range(GROUP)], axis=0)
-            query_ref[i] = stack.T.astype(BF16)
+            query_ref[i, :, : GROUP * size] = stack.T.astype(BF16)
+
+        def whole_block(i, _):
+            gather_block(QUERY_BLOCK, i)
             return 0
 
-        lax.fori_loop(0, count, gather_block, 0)
+        lax.fori_loop(0, count, whole_block, 0)
+        pl.when(odd)(functools.partial(gather_block, HALF_BLOCK, count))
         end = offset + total
 
         def turn_block(b, _):
@@ -147,39 +153,45 @@
         key_blocks = (end + KEY_BLOCK - 1) // KEY_BLOCK
         lax.fori_loop(offset // KEY_BLOCK, key_blocks, turn_block, 0)
 
-        def attend_block(i, used):
-            at = pl.ds(pl.multiple_of(i * QUERY_BLOCK, QUERY_BLOCK), QUERY_BLOCK)
+        def attend_block(size, i, used):
+            lanes = GROUP * size
+            query = query_ref[i, :, :lanes]
+            at = pl.ds(pl.multiple_of(i * QUERY_BLOCK, HALF_BLOCK), size)
             top = jnp.full((1, lanes), -1e30, F32)
             for b in range(used):
                 part = slice(b * KEY_BLOCK, (b + 1) * KEY_BLOCK)
                 bias = jnp.concatenate([bias_ref[part, :]] * (lanes // HD), axis=1)
-                scores = jnp.dot(k_ref[part, :], query_ref[i], preferred_element_type=F32) * factor + bias
-                score_ref[part, :] = scores
+                scores = jnp.dot(k_ref[part, :], query, preferred_element_type=F32) * factor + bias
+                score_ref[part, :lanes] = scores
                 top = jnp.maximum(top, jnp.max(scores, axis=0, keepdims=True))
             total = jnp.zeros((1, lanes), F32)
             accum = jnp.zeros((HD, lanes), F32)
             for b in range(used):
                 part = slice(b * KEY_BLOCK, (b + 1) * KEY_BLOCK)
-                weights = jnp.exp2(score_ref[part, :] - top)
+                weights = jnp.exp2(score_ref[part, :lanes] - top)
                 total = total + jnp.sum(weights, axis=0, keepdims=True)
                 accum = accum + jnp.dot(turned_ref[:, part], weights.astype(BF16), preferred_element_type=F32)
             result = (accum / total).T.astype(BF16)
             for h in range(GROUP):
-                held_ref[at, h * HD : (h + 1) * HD] = result[h * QUERY_BLOCK : (h + 1) * QUERY_BLOCK]
+                held_ref[at, h * HD : (h + 1) * HD] = result[h * size : (h + 1) * size]
+
+        def by_keys(size, i):
+            for used in range(1, turned_ref.shape[1] // KEY_BLOCK + 1):
+                pl.when(key_blocks == used)(functools.partial(attend_block, size, i, used))
 
         def query_step(i, _):
-            for used in range(1, turned_ref.shape[1] // KEY_BLOCK + 1):
-                pl.when(key_blocks == used)(functools.partial(attend_block, i, used))
+            by_keys(QUERY_BLOCK, i)
             return 0
 
         lax.fori_loop(0, count, query_step, 0)
+        pl.when(odd)(functools.partial(by_keys, HALF_BLOCK, count))
 
         def clear_block(i, _):
-            at = pl.ds(pl.multiple_of(i * QUERY_BLOCK, QUERY_BLOCK), QUERY_BLOCK)
-            held_ref[at, :] = jnp.zeros((QUERY_BLOCK, BACK), BF16)
+            at = pl.ds(pl.multiple_of(i * HALF_BLOCK, HALF_BLOCK), HALF_BLOCK)
+            held_ref[at, :] = jnp.zeros((HALF_BLOCK, BACK), BF16)
             return 0
 
-        lax.fori_loop(count, blocks, clear_block, 0)
+        lax.fori_loop(halves, blocks * QUERY_BLOCK // HALF_BLOCK, clear_block, 0)
         slots = blocks * QUERY_BLOCK
         wide = jnp.concatenate([down] * (-(-slots // HD)), axis=1)[:, :slots]
         unfold = one_hot(wide == iota((rows, slots), 1).astype(F32))

time: 218 us -> 218 us (level)
    all_to_all x2, blocking collectives: 188 us -> 186 us  [exchange(): lax.all_to_all(shaped, ('span', 'seq'), split_axis=0, concat_axis=0, tile...]
where the time goes in v1:
time: 218 us; the launch traced here: 215 us
  blocking collectives  186 us (85%)
  Pallas kernels  29.7 us (14%)
    all_to_all x2, blocking collectives, exchange(): lax.all_to_all(shaped, ('span', 'seq'), split_axis=0, concat_axis=0, tile...  186 us
    pallas_call x1, Pallas kernels, attend(): call(attend_kernel, 'attend', jax.ShapeDtypeStruct((spans * rows, BACK),...  22.4 us
    pallas_call x1, Pallas kernels, local(): call(pack_kernel, 'pack', shape((KVH * rows, WIDE), BF16), 4 * rows * row...  5.03 us

profile of v1, /device:TPU:7, one launch (start us, length us, event | category | flops | bytes accessed | tf_op | source)
XLA Modules:
  0.0 215.4 jit_solution(5531498420352023415)
XLA Ops:
  0.0 5.0 %pack.1 = bf16[2048,896]{1,0:T(8,128)(2,1)} custom-call(s32[1,224]{1,0:T(1,128)} %owner_ref.3, bf16[224,3072]{1,0:T(8,128)(2,1)} %bitcast.12, bf16[224,512]{1,0:T(8,128)(2,1)} %bitcast.13, bf16[224,512]{1,0:T(8,128)(2,1)} %bitcast.14), custom_call_target="tpu_custom_call" | custom-call | flops 1409286144 | bytes 3670016 | tf_op jit(solution)/shard_map/pack/pallas_call | solution.py:265
  5.0 101.8 %all_to_all.10 = bf16[256,8,896]{2,1,0:T(8,128)(2,1)} all-to-all(bf16[256,8,896]{2,1,0:T(8,128)(2,1)} %bitcast.10), channel_id=1, replica_groups=mesh['span'=4,'seq'=64] {'span','seq'}, dimensions={0} | all-to-all | bytes 7340032 | tf_op jit(solution)/shard_map/all_to_all | solution.py:229
  106.9 22.4 %attend.1 = bf16[2048,768]{1,0:T(8,128)(2,1)S(1)} custom-call(bf16[2048,896]{1,0:T(8,128)(2,1)} %bitcast.11), custom_call_target="tpu_custom_call" | custom-call | flops 9865003008 | bytes 7340032 | tf_op jit(solution)/shard_map/attend/pallas_call | solution.py:237
  129.3 0.0 copy-start
  129.4 83.8 %all_to_all.11 = bf16[256,8,768]{2,1,0:T(8,128)(2,1)S(1)} all-to-all(bf16[256,8,768]{2,1,0:T(8,128)(2,1)S(1)} %bitcast.9), channel_id=1, replica_groups=mesh['span'=4,'seq'=64] {'span','seq'}, dimensions={0} | all-to-all | bytes 6291456 | tf_op jit(solution)/shard_map/all_to_all | solution.py:229
  213.2 0.0 copy-done
  213.2 2.2 %unpack.1 = bf16[224,3072]{1,0:T(8,128)(2,1)} custom-call(s32[1,224]{1,0:T(1,128)S(1)} %copy-done, bf16[2048,768]{1,0:T(8,128)(2,1)S(1)} %bitcast.8), custom_call_target="tpu_custom_call" | custom-call | flops 704643072 | bytes 6291456 | tf_op jit(solution)/shard_map/unpack/pallas_call | solution.py:284
Async XLA Ops:
  129.3 83.9 %copy-start = (s32[1,224]{1,0:T(1,128)S(1)}, s32[1,224]{1,0:T(1,128)}, u32[]{:S(2)}) copy-start(s32[1,224]{1,0:T(1,128)} %owner_ref.3) | copy-start | bytes 2692

commit v2 on v1

--- a/solution.py
+++ b/solution.py
@@ -16,6 +16,10 @@
 SLOTS = 7
 WIDE = SLOTS * HD
 BACK = GROUP * HD
+FOUR = 4
+LATE = SLOTS - FOUR
+SIDE = (GROUP - 1) * HD
+RETURNED = BACK + SIDE
 KEY_BLOCK = 256
 QUERY_BLOCK = 128
 HALF_BLOCK = QUERY_BLOCK // 2
@@ -93,6 +97,21 @@
     return tail.reshape(tiles * TILE, HD)
 
 
+def returned_places(flags, first):
+    rows = flags.shape[0]
+    shape = (rows // TILE * FOUR, rows)
+    line = iota(shape, 0)
+    row = (line // FOUR) * TILE + (line & (FOUR - 1)) + first
+    ahead = jnp.dot(one_hot(iota(shape, 1) < row), flags, preferred_element_type=F32)
+    held = jnp.dot(one_hot(iota(shape, 1) == row), flags, preferred_element_type=F32)
+    return jnp.where(held > 0.5, ahead, -1.0)
+
+
+def picks(place, slots):
+    wide = jnp.concatenate([place] * (slots // HD), axis=1)
+    return one_hot(wide == iota(wide.shape, 1).astype(F32))
+
+
 def attend_kernel(
     got_ref, out_ref, x_ref, before_ref, k_ref, v_ref, turned_ref, bias_ref, query_ref, held_ref, score_ref, sem
 ):
@@ -193,10 +212,21 @@
 
         lax.fori_loop(halves, blocks * QUERY_BLOCK // HALF_BLOCK, clear_block, 0)
         slots = blocks * QUERY_BLOCK
-        wide = jnp.concatenate([down] * (-(-slots // HD)), axis=1)[:, :slots]
-        unfold = one_hot(wide == iota((rows, slots), 1).astype(F32))
-        moved = jnp.dot(unfold, held_ref[...], preferred_element_type=F32)
-        out_ref[pl.ds(pl.multiple_of(t * rows, rows), rows), :] = moved.astype(BF16)
+        flags = one_hot(valid)
+        early = returned_places(flags, 0)
+        late = returned_places(flags, FOUR)
+        last = (iota((early.shape[0], HD), 0) & (FOUR - 1)) == FOUR - 1
+        at = pl.ds(pl.multiple_of(t * (rows // TILE), rows // TILE), rows // TILE)
+        moved = jnp.dot(picks(early, slots), held_ref[...], preferred_element_type=F32)
+        out_ref[at, :, :BACK] = moved.astype(BF16).reshape(rows // TILE, FOUR, BACK)
+        moved = jnp.dot(picks(late, slots), held_ref[:, :SIDE], preferred_element_type=F32)
+        for j in range(GROUP - 1):
+            piece = moved[:, j * HD : (j + 1) * HD]
+            if j < LATE:
+                place = jnp.where(last, pltpu.roll(late, FOUR - 1 - j, 0), -1.0)
+                piece = piece + jnp.dot(picks(place, slots), held_ref[:, SIDE:], preferred_element_type=F32)
+            lane = BACK + j * HD
+            out_ref[at, :, lane : lane + HD] = piece.astype(BF16).reshape(rows // TILE, FOUR, HD)
         return offset + (total + ALIGN - 1) // ALIGN * ALIGN
 
     lax.fori_loop(0, spans, span_step, jnp.int32(0))
@@ -205,11 +235,23 @@
 def unpack_kernel(owner_ref, got_ref, out_ref):
     owner, rank = row_ranks(owner_ref, 1)
     count = owner.shape[0]
-    rows = got_ref.shape[0] // KVH
-    pick = one_hot(iota((count, rows), 1) == owner * TILE + rank)
+    owners = got_ref.shape[0] // KVH
+    lines = owners * FOUR
+    line = iota((count, lines), 1)
+    early = one_hot((line == owner * FOUR + rank) & (rank < FOUR))
+    late = one_hot((line == owner * FOUR + rank - FOUR) & (rank >= FOUR))
+    aside = line == owner * FOUR + FOUR - 1
     for c in range(KVH):
-        moved = jnp.dot(pick, got_ref[c * rows : (c + 1) * rows, :], preferred_element_type=F32)
-        out_ref[:, c * BACK : (c + 1) * BACK] = moved.astype(BF16)
+        part = got_ref[c * owners : (c + 1) * owners].reshape(lines, RETURNED)
+        moved = jnp.dot(early, part[:, :BACK], preferred_element_type=F32)
+        more = jnp.dot(late, part[:, BACK:], preferred_element_type=F32)
+        out_ref[:, c * BACK : c * BACK + SIDE] = (moved[:, :SIDE] + more).astype(BF16)
+        sixth = moved[:, SIDE:]
+        for s in range(LATE):
+            lane = BACK + s * HD
+            chosen = one_hot(aside & (rank == FOUR + s))
+            sixth = sixth + jnp.dot(chosen, part[:, lane : lane + HD], preferred_element_type=F32)
+        out_ref[:, c * BACK + SIDE : (c + 1) * BACK] = sixth.astype(BF16)
 
 
 def call(kernel, name, out_shape, flops, moved, scratch=(), limit=VMEM_LIMIT, **specs):
@@ -224,9 +266,8 @@
     )
 
 
-def exchange(rows):
-    shaped = rows.reshape(rows.shape[0] // TILE, TILE, rows.shape[1])
-    return lax.all_to_all(shaped, ("span", "seq"), split_axis=0, concat_axis=0, tiled=True).reshape(rows.shape)
+def exchange(chunks):
+    return lax.all_to_all(chunks, ("span", "seq"), split_axis=0, concat_axis=0, tiled=True)
 
 
 def attend(got, owners, spans):
@@ -237,7 +278,7 @@
     return call(
         attend_kernel,
         "attend",
-        jax.ShapeDtypeStruct((spans * rows, BACK), BF16),
+        jax.ShapeDtypeStruct((spans * owners, FOUR, RETURNED), BF16),
         4 * own_rows * own_rows * spans * spans * HD * GROUP,
         4 * spans * rows * WIDE,
         [
@@ -280,7 +321,8 @@
         in_specs=[pl.BlockSpec(memory_space=pltpu.VMEM)] + [pl.BlockSpec(memory_space=pl.ANY)] * 3,
         out_specs=pl.BlockSpec(memory_space=pl.ANY),
     )(owner_ids, query_rows[0], key_rows[0], value_rows[0])
-    done = attend(exchange(send), owners, spans)
+    got = exchange(send.reshape(KVH * owners, TILE, WIDE)).reshape(spans * rows, WIDE)
+    done = attend(got, owners, spans)
     result = call(
         unpack_kernel,
         "unpack",

time: 218 us -> 214 us (0.982)
  blocking collectives: 186 us -> 177 us
  Pallas kernels: 29.7 us -> 34.7 us
    all_to_all x2, blocking collectives: 186 us -> 177 us  [exchange(): lax.all_to_all(chunks, ('span', 'seq'), split_axis=0, concat_axis=0, tile...]
    pallas_call x1, Pallas kernels: 22.4 us -> 27 us  [attend(): call(attend_kernel, 'attend', jax.ShapeDtypeStruct((spans * owners, FOUR,...]
where the time goes in v2:
time: 214 us; the launch traced here: 211 us
  blocking collectives  177 us (83%)
  Pallas kernels  34.7 us (16%)
    all_to_all x2, blocking collectives, exchange(): lax.all_to_all(chunks, ('span', 'seq'), split_axis=0, concat_axis=0, tile...  177 us
    pallas_call x1, Pallas kernels, attend(): call(attend_kernel, 'attend', jax.ShapeDtypeStruct((spans * owners, FOUR,...  27 us
    pallas_call x1, Pallas kernels, local(): call(pack_kernel, 'pack', shape((KVH * rows, WIDE), BF16), 4 * rows * row...  5.03 us

profile of v2, /device:TPU:7, one launch (start us, length us, event | category | flops | bytes accessed | tf_op | source)
XLA Modules:
  0.0 211.3 jit_solution(11101672992414345609)
XLA Ops:
  0.0 5.0 %pack.1 = bf16[2048,896]{1,0:T(8,128)(2,1)} custom-call(s32[1,224]{1,0:T(1,128)} %owner_ref.3, bf16[224,3072]{1,0:T(8,128)(2,1)} %bitcast.8, bf16[224,512]{1,0:T(8,128)(2,1)} %bitcast.9, bf16[224,512]{1,0:T(8,128)(2,1)} %bitcast.10), custom_call_target="tpu_custom_call" | custom-call | flops 1409286144 | bytes 3670016 | tf_op jit(solution)/shard_map/pack/pallas_call | solution.py:306
  5.0 101.8 %all_to_all.10 = bf16[256,8,896]{2,1,0:T(8,128)(2,1)} all-to-all(bf16[256,8,896]{2,1,0:T(8,128)(2,1)} %bitcast.6), channel_id=1, replica_groups=mesh['span'=4,'seq'=64] {'span','seq'}, dimensions={0} | all-to-all | bytes 7340032 | tf_op jit(solution)/shard_map/all_to_all | solution.py:270
  106.9 27.0 %attend.1 = bf16[256,4,1408]{2,1,0:T(4,128)(2,1)S(1)} custom-call(bf16[2048,896]{1,0:T(8,128)(2,1)} %bitcast.7), custom_call_target="tpu_custom_call" | custom-call | flops 9865003008 | bytes 7340032 | tf_op jit(solution)/shard_map/attend/pallas_call | solution.py:278
  133.9 0.0 copy-start
  133.9 74.7 %all_to_all.11.got_ref = bf16[256,4,1408]{2,1,0:T(4,128)(2,1)S(1)} all-to-all(bf16[256,4,1408]{2,1,0:T(4,128)(2,1)S(1)} %attend.1), channel_id=1, replica_groups=mesh['span'=4,'seq'=64] {'span','seq'}, dimensions={0} | all-to-all | bytes 5767168 | tf_op jit(solution)/shard_map/all_to_all | solution.py:270
  208.6 0.0 copy-done
  208.6 2.6 %unpack.1 = bf16[224,3072]{1,0:T(8,128)(2,1)} custom-call(s32[1,224]{1,0:T(1,128)S(1)} %copy-done, bf16[256,4,1408]{2,1,0:T(4,128)(2,1)S(1)} %all_to_all.11.got_ref), custom_call_target="tpu_custom_call" | custom-call | flops 704643072 | bytes 6291456 | tf_op jit(solution)/shard_map/unpack/pallas_call | solution.py:326
Async XLA Ops:
  133.9 74.7 %copy-start = (s32[1,224]{1,0:T(1,128)S(1)}, s32[1,224]{1,0:T(1,128)}, u32[]{:S(2)}) copy-start(s32[1,224]{1,0:T(1,128)} %owner_ref.3) | copy-start | bytes 2692

commit v3 on v2

--- a/solution.py
+++ b/solution.py
@@ -177,16 +177,16 @@
             query = query_ref[i, :, :lanes]
             at = pl.ds(pl.multiple_of(i * QUERY_BLOCK, HALF_BLOCK), size)
             top = jnp.full((1, lanes), -1e30, F32)
-            for b in range(used):
-                part = slice(b * KEY_BLOCK, (b + 1) * KEY_BLOCK)
+            for b in range(0, used, 2):
+                part = slice(b * KEY_BLOCK, min(b + 2, used) * KEY_BLOCK)
                 bias = jnp.concatenate([bias_ref[part, :]] * (lanes // HD), axis=1)
                 scores = jnp.dot(k_ref[part, :], query, preferred_element_type=F32) * factor + bias
                 score_ref[part, :lanes] = scores
                 top = jnp.maximum(top, jnp.max(scores, axis=0, keepdims=True))
             total = jnp.zeros((1, lanes), F32)
             accum = jnp.zeros((HD, lanes), F32)
-            for b in range(used):
-                part = slice(b * KEY_BLOCK, (b + 1) * KEY_BLOCK)
+            for b in range(0, used, 2):
+                part = slice(b * KEY_BLOCK, min(b + 2, used) * KEY_BLOCK)
                 weights = jnp.exp2(score_ref[part, :lanes] - top)
                 total = total + jnp.sum(weights, axis=0, keepdims=True)
                 accum = accum + jnp.dot(turned_ref[:, part], weights.astype(BF16), preferred_element_type=F32)
@@ -219,12 +219,12 @@
         at = pl.ds(pl.multiple_of(t * (rows // TILE), rows // TILE), rows // TILE)
         moved = jnp.dot(picks(early, slots), held_ref[...], preferred_element_type=F32)
         out_ref[at, :, :BACK] = moved.astype(BF16).reshape(rows // TILE, FOUR, BACK)
-        moved = jnp.dot(picks(late, slots), held_ref[:, :SIDE], preferred_element_type=F32)
+        moved = jnp.dot(picks(late, slots), held_ref[...], preferred_element_type=F32)
+        sixth = moved[:, SIDE:]
         for j in range(GROUP - 1):
             piece = moved[:, j * HD : (j + 1) * HD]
             if j < LATE:
-                place = jnp.where(last, pltpu.roll(late, FOUR - 1 - j, 0), -1.0)
-                piece = piece + jnp.dot(picks(place, slots), held_ref[:, SIDE:], preferred_element_type=F32)
+                piece = jnp.where(last, pltpu.roll(sixth, FOUR - 1 - j, 0), piece)
             lane = BACK + j * HD
             out_ref[at, :, lane : lane + HD] = piece.astype(BF16).reshape(rows // TILE, FOUR, HD)
         return offset + (total + ALIGN - 1) // ALIGN * ALIGN

time: 214 us -> 214 us (level)
  no operation moved by 1% of the time
where the time goes in v3:
time: 214 us; the launch traced here: 210 us
  blocking collectives  178 us (83%)
  Pallas kernels  32.7 us (15%)
    all_to_all x2, blocking collectives, exchange(): lax.all_to_all(chunks, ('span', 'seq'), split_axis=0, concat_axis=0, tile...  178 us
    pallas_call x1, Pallas kernels, attend(): call(attend_kernel, 'attend', jax.ShapeDtypeStruct((spans * owners, FOUR,...  25.1 us
    pallas_call x1, Pallas kernels, local(): call(pack_kernel, 'pack', shape((KVH * rows, WIDE), BF16), 4 * rows * row...  5.03 us

profile of v3, /device:TPU:7, one launch (start us, length us, event | category | flops | bytes accessed | tf_op | source)
XLA Modules:
  0.0 210.3 jit_solution(11211795605868715585)
XLA Ops:
  0.0 5.0 %pack.1 = bf16[2048,896]{1,0:T(8,128)(2,1)} custom-call(s32[1,224]{1,0:T(1,128)} %owner_ref.3, bf16[224,3072]{1,0:T(8,128)(2,1)} %bitcast.8, bf16[224,512]{1,0:T(8,128)(2,1)} %bitcast.9, bf16[224,512]{1,0:T(8,128)(2,1)} %bitcast.10), custom_call_target="tpu_custom_call" | custom-call | flops 1409286144 | bytes 3670016 | tf_op jit(solution)/shard_map/pack/pallas_call | solution.py:306
  5.0 101.8 %all_to_all.10 = bf16[256,8,896]{2,1,0:T(8,128)(2,1)} all-to-all(bf16[256,8,896]{2,1,0:T(8,128)(2,1)} %bitcast.6), channel_id=1, replica_groups=mesh['span'=4,'seq'=64] {'span','seq'}, dimensions={0} | all-to-all | bytes 7340032 | tf_op jit(solution)/shard_map/all_to_all | solution.py:270
  106.9 25.1 %attend.1 = bf16[256,4,1408]{2,1,0:T(4,128)(2,1)S(1)} custom-call(bf16[2048,896]{1,0:T(8,128)(2,1)} %bitcast.7), custom_call_target="tpu_custom_call" | custom-call | flops 9865003008 | bytes 7340032 | tf_op jit(solution)/shard_map/attend/pallas_call | solution.py:278
  132.0 0.0 copy-start
  132.0 75.7 %all_to_all.11.got_ref = bf16[256,4,1408]{2,1,0:T(4,128)(2,1)S(1)} all-to-all(bf16[256,4,1408]{2,1,0:T(4,128)(2,1)S(1)} %attend.1), channel_id=1, replica_groups=mesh['span'=4,'seq'=64] {'span','seq'}, dimensions={0} | all-to-all | bytes 5767168 | tf_op jit(solution)/shard_map/all_to_all | solution.py:270
  207.7 0.0 copy-done
  207.7 2.6 %unpack.1 = bf16[224,3072]{1,0:T(8,128)(2,1)} custom-call(s32[1,224]{1,0:T(1,128)S(1)} %copy-done, bf16[256,4,1408]{2,1,0:T(4,128)(2,1)S(1)} %all_to_all.11.got_ref), custom_call_target="tpu_custom_call" | custom-call | flops 704643072 | bytes 6291456 | tf_op jit(solution)/shard_map/unpack/pallas_call | solution.py:326
Async XLA Ops:
  132.0 75.7 %copy-start = (s32[1,224]{1,0:T(1,128)S(1)}, s32[1,224]{1,0:T(1,128)}, u32[]{:S(2)}) copy-start(s32[1,224]{1,0:T(1,128)} %owner_ref.3) | copy-start | bytes 2692
